TPU v7x, 32 devices: a whole 2x2x4 slice. The times are simulated.
32 devices in a mesh: src: 4 (over y, x), tgt: 8 (over z, core).
Axes of the slice: x: 2, y: 2, z: 4, core: 2. Of those that a mesh axis runs over, the one named last changes fastest.
Arguments:
- source_values: float32 [16, 65536], P(None, ('src', 'tgt')), may hold values from -6 to 6
- source_phase: float32 [65536], P(('src', 'tgt')), may hold values from -3.140625 to 3.140625
- leaf_interp: bfloat16 [64, 64], replicated, may hold values from -0.75 to 0.75
- level_interp: bfloat16 [11, 2, 64, 64], replicated, may hold values from -0.5 to 0.5
- level_phase: float32 [11, 3, 1024, 64], P(None, None, ('src', 'tgt')), may hold values from -3.140625 to 3.140625
- middle_interp: bfloat16 [64, 64], replicated, may hold values from -0.75 to 0.75
- middle_phase: float32 [2, 1024, 64], P(None, ('src', 'tgt')), may hold values from -3.140625 to 3.140625
- final_phase: float32 [1024, 64], P(('src', 'tgt')), may hold values from -3.140625 to 3.140625
- final_interp: bfloat16 [64, 64], replicated, may hold values from -0.75 to 0.75
- target_phase: float32 [65536], P(('src', 'tgt')), may hold values from -3.140625 to 3.140625
Outputs:
- target_values: float32 [2, 16, 65536], P(None, None, ('src', 'tgt'))
All inputs are finite; a program needn't handle non-finite values.
Results may differ from a plain program's by a relative error of at most 0.024.
Values may be sent and summed in bfloat16 or wider, within the bound.
A program may use at most 64 MiB of HBM per device.

v0:
```python
import jax
import jax.numpy as jnp
from jax import lax
from jax.sharding import PartitionSpec as P

LOCAL_SRC = 3
LOCAL_TGT = 3


def swapped(shard, axis, stride):
    return lax.ppermute(shard, axis, [(i, i ^ 1 << stride) for i in range(lax.axis_size(axis))])


def rotate(vectors, angles):
    half_width = angles.shape[-1]
    values = vectors.astype(jnp.float32)
    real_part = values[..., :half_width]
    imag_part = values[..., half_width:]
    cosine = jnp.cos(angles)[:, None, :]
    sine_val = jnp.sin(angles)[:, None, :]
    return jnp.concatenate(
        [real_part * cosine - imag_part * sine_val, real_part * sine_val + imag_part * cosine], -1
    )


def block_pair(matrix):
    zeros_block = jnp.zeros_like(matrix)
    upper_rows = jnp.concatenate([matrix, zeros_block], 1)
    lower_rows = jnp.concatenate([zeros_block, matrix], 1)
    return jnp.concatenate([upper_rows, lower_rows], 0)


def flip_pairs(coeffs, stride):
    shape = coeffs.shape
    return coeffs.reshape((shape[0] // (2 * stride), 2, stride) + shape[1:])[:, ::-1].reshape(shape)


def translate(coeffs, partner, phases, matrices):
    shape = coeffs.shape
    own_rot = rotate(coeffs, phases[0]).astype(jnp.bfloat16).reshape(-1, shape[2])
    other_rot = rotate(partner, phases[1]).astype(jnp.bfloat16).reshape(-1, shape[2])
    joined = jnp.concatenate([own_rot, other_rot], 1)
    weights = jnp.concatenate([block_pair(matrices[0]), block_pair(matrices[1])], 0)
    summed = jnp.dot(joined, weights, preferred_element_type=jnp.float32)
    return rotate(summed.reshape(shape), phases[2]).astype(jnp.bfloat16)


def shards(
    source_values,
    source_phase,
    leaf_interp,
    level_interp,
    level_phase,
    middle_interp,
    middle_phase,
    final_phase,
    final_interp,
    target_phase,
):
    blocks = level_phase.shape[2]
    rhs_count = source_values.shape[0]
    leaf_size = leaf_interp.shape[0]
    rank_size = leaf_interp.shape[1]
    width = 2 * rank_size
    src_count = lax.axis_size("src")
    tgt_count = lax.axis_size("tgt")
    src_bits = src_count.bit_length() - 1
    tgt_bits = tgt_count.bit_length() - 1
    cos_src = jnp.cos(source_phase)[None, :]
    sin_src = jnp.sin(source_phase)[None, :]
    modulated = jnp.stack([source_values * cos_src, -source_values * sin_src]).astype(jnp.bfloat16)
    modulated = modulated.reshape(2, rhs_count, blocks, leaf_size)
    leaf_terms = jnp.einsum(
        "csbj,jk->bsck", modulated, leaf_interp, preferred_element_type=jnp.float32
    )
    coeffs = leaf_terms.reshape(blocks, rhs_count, width).astype(jnp.bfloat16)
    level_index = 0
    for step_index in range(LOCAL_SRC):
        partner = flip_pairs(coeffs, 2**step_index)
        coeffs = translate(coeffs, partner, level_phase[level_index], level_interp[level_index])
        level_index += 1
    for bit_index in range(src_bits):
        partner = swapped(coeffs, "src", bit_index)
        coeffs = translate(coeffs, partner, level_phase[level_index], level_interp[level_index])
        level_index += 1
    regrouped = lax.all_to_all(coeffs, ("src", "tgt"), split_axis=0, concat_axis=0, tiled=True)
    switched = rotate(regrouped, middle_phase[0]).astype(jnp.bfloat16).reshape(-1, width)
    middle_sum = jnp.dot(switched, block_pair(middle_interp), preferred_element_type=jnp.float32)
    coeffs = rotate(middle_sum.reshape(blocks, rhs_count, width), middle_phase[1]).astype(
        jnp.bfloat16
    )
    for bit_index in range(tgt_bits):
        partner = swapped(coeffs, "tgt", bit_index)
        coeffs = translate(coeffs, partner, level_phase[level_index], level_interp[level_index])
        level_index += 1
    for step_index in range(LOCAL_TGT):
        partner = flip_pairs(coeffs, 2**step_index)
        coeffs = translate(coeffs, partner, level_phase[level_index], level_interp[level_index])
        level_index += 1
    finals = (
        rotate(coeffs, final_phase).astype(jnp.bfloat16).reshape(blocks, rhs_count, 2, rank_size)
    )
    evaluated = jnp.einsum(
        "bsck,kj->csbj", finals, final_interp, preferred_element_type=jnp.float32
    )
    evaluated = evaluated.reshape(2, rhs_count, blocks * leaf_size)
    cos_tgt = jnp.cos(target_phase)[None, :]
    sin_tgt = jnp.sin(target_phase)[None, :]
    real_out = evaluated[0] * cos_tgt - evaluated[1] * sin_tgt
    imag_out = evaluated[0] * sin_tgt + evaluated[1] * cos_tgt
    return jnp.stack([real_out, imag_out])


def solution(mesh):
    return jax.shard_map(
        shards,
        mesh=mesh,
        in_specs=(
            P(None, ("src", "tgt")),
            P(("src", "tgt")),
            P(),
            P(),
            P(None, None, ("src", "tgt"), None),
            P(),
            P(None, ("src", "tgt"), None),
            P(("src", "tgt"), None),
            P(),
            P(("src", "tgt")),
        ),
        out_specs=P(None, None, ("src", "tgt")),
        check_vma=False,
    )
```

profile of v0, /device:TPU:0, one launch (start us, length us, event | category | flops | bytes accessed | tf_op | source)
XLA Modules:
  0.0 61.5 jit_solution(3362876280130293711)
XLA Ops:
  0.0 1.9 %cosine_bitcast_fusion = (f32[32,64]{1,0:T(8,128)S(1)}, f32[32,64]{1,0:T(8,128)S(1)}, f32[32,64]{1,0:T(8,128)S(1)}, f32[32,64]{1,0:T(8,128)S(1)}, f32[32,64]{1,0...) fusion(f32[11,3,32,64]{3,2,1,0:T(8,128)} %param.14), kind=kLoop, calls=%fused_computation.378 | loop fusion | bytes 311296 | tf_op jit(solution)/shard_map/cos | solution.py:19
  2.0 0.5 cosine_bitcast_fusion.26
  4.1 0.7 %copy-done.2 = bf16[11,2,64,64]{3,2,1,0:T(8,128)(2,1)S(1)} copy-done((bf16[11,2,64,64]{3,2,1,0:T(8,128)(2,1)S(1)}, bf16[11,2,64,64]{3,2,1,0:T(8,128)(2,1)}, u32[]{:S(2)}) %copy-start.2) | copy-done | bytes 180248
  5.7 0.3 fusion.4
  6.8 0.3 fusion.12
  7.9 0.3 fusion.20
  8.5 3.0 %collective-permute-start = (bf16[32,16,128]{2,1,0:T(8,128)(2,1)S(1)}, bf16[32,16,128]{2,1,0:T(8,128)(2,1)S(1)}, u32[]{:S(2)}, u32[]{:S(2)}) collective-permute-start(bf16[32,16,128]{2,1,0:T(8,128)(2,1)S(1)} %get-tuple-element.14), channel_id=1, source_target_pairs={{0,8},{8,0},{16,24},{24,16},{1,9},{9,1},{17,25},{25,17},{2,10},{10... | collective-permute-start | bytes 393224 | tf_op jit(solution)/shard_map/ppermute | solution.py:11
  11.5 1.0 %cosine_bitcast_fusion.1 = (f32[32,64]{1,0:T(8,128)S(1)}, f32[32,64]{1,0:T(8,128)S(1)}, f32[32,64]{1,0:T(8,128)S(1)}, f32[32,64]{1,0:T(8,128)S(1)}, f32[32,64]{1...) fusion(f32[11,3,32,64]{3,2,1,0:T(8,128)S(1)} %copy-done.1), kind=kLoop, calls=%fused_computation.382 | loop fusion | bytes 311296 | tf_op jit(solution)/shard_map/cos | solution.py:19
  12.9 0.5 copy-done.5
  13.5 1.6 %collective-permute-done = bf16[32,16,128]{2,1,0:T(8,128)(2,1)S(1)} collective-permute-done((bf16[32,16,128]{2,1,0:T(8,128)(2,1)S(1)}, bf16[32,16,128]{2,1,0:T(8,128)(2,1)S(1)}, u32[]{:S(2)}, u32[]{:S(2)}) %collective-permute-start) | collective-permute-done | bytes 131104 | tf_op jit(solution)/shard_map/ppermute | solution.py:11
  15.3 0.3 fusion.28
  15.9 1.8 %collective-permute-start.1 = (bf16[32,16,128]{2,1,0:T(8,128)(2,1)S(1)}, bf16[32,16,128]{2,1,0:T(8,128)(2,1)S(1)}, u32[]{:S(2)}, u32[]{:S(2)}) collective-permute-start(bf16[32,16,128]{2,1,0:T(8,128)(2,1)S(1)} %get-tuple-element.12), channel_id=1, source_target_pairs={{0,16},{8,24},{16,0},{24,8},{1,17},{9,25},{17,1},{25,9},{2,18},{10... | collective-permute-start | bytes 393224 | tf_op jit(solution)/shard_map/ppermute | solution.py:11
  17.9 3.0 %collective-permute-done.1 = bf16[32,16,128]{2,1,0:T(8,128)(2,1)S(1)} collective-permute-done((bf16[32,16,128]{2,1,0:T(8,128)(2,1)S(1)}, bf16[32,16,128]{2,1,0:T(8,128)(2,1)S(1)}, u32[]{:S(2)}, u32[]{:S(2)}) %collective-permute-start.1) | collective-permute-done | bytes 131104 | tf_op jit(solution)/shard_map/ppermute | solution.py:11
  21.1 0.3 fusion.36
  21.6 0.8 %pad_maximum_fusion.5 = bf16[32,16,128]{2,1,0:T(8,128)(2,1)} fusion(bf16[32,16,64]{2,1,0:T(8,128)(2,1)S(1)} %get-tuple-element.148, bf16[32,16,64]{2,1,0:T(8,128)(2,1)S(1)} %get-tuple-element.147), kind=kLoop, calls=%fused_computation.206 | loop fusion | flops 262144 | bytes 262144 | tf_op jit(solution)/shard_map/concatenate | solution.py:21
  22.4 6.3 %all-to-all-start = ((bf16[32,16,128]{2,1,0:T(8,128)(2,1)}), bf16[32,16,128]{2,1,0:T(8,128)(2,1)S(1)}, u32[]{:S(2)}, u32[]{:S(2)}) async-start(bf16[32,16,128]{2,1,0:T(8,128)(2,1)} %pad_maximum_fusion.5), calls=%async_computation | async-start | bytes 262144 | tf_op jit(solution)/shard_map/all_to_all | solution.py:86
  28.7 0.8 %sine_bitcast_fusion = (f32[32,64]{1,0:T(8,128)S(1)}, f32[32,64]{1,0:T(8,128)S(1)}, f32[32,64]{1,0:T(8,128)S(1)}, f32[32,64]{1,0:T(8,128)S(1)}, f32[32,64]{1,0:T...) fusion(f32[11,3,32,64]{3,2,1,0:T(8,128)S(1)} %copy-done.1), kind=kLoop, calls=%fused_computation.377 | loop fusion | bytes 278528 | tf_op jit(solution)/shard_map/sin | solution.py:20
  29.6 7.1 %all-to-all-done = bf16[32,16,128]{2,1,0:T(8,128)(2,1)S(1)} async-done(((bf16[32,16,128]{2,1,0:T(8,128)(2,1)}), bf16[32,16,128]{2,1,0:T(8,128)(2,1)S(1)}, u32[]{:S(2)}, u32[]{:S(2)}) %all-to-all-start) | async-done | bytes 131104 | tf_op jit(solution)/shard_map/all_to_all | solution.py:86
  36.9 0.5 copy-done.6
  38.0 0.4 collective-permute-start.2
  38.5 0.9 %collective-permute-done.2 = bf16[32,16,128]{2,1,0:T(8,128)(2,1)S(1)} collective-permute-done((bf16[32,16,128]{2,1,0:T(8,128)(2,1)S(1)}, bf16[32,16,128]{2,1,0:T(8,128)(2,1)S(1)}, u32[]{:S(2)}, u32[]{:S(2)}) %collective-permute-start.2) | collective-permute-done | bytes 131104 | tf_op jit(solution)/shard_map/ppermute | solution.py:11
  39.6 0.3 fusion.44
  40.2 0.5 collective-permute-start.3
  40.9 5.0 %collective-permute-done.3 = bf16[32,16,128]{2,1,0:T(8,128)(2,1)S(1)} collective-permute-done((bf16[32,16,128]{2,1,0:T(8,128)(2,1)S(1)}, bf16[32,16,128]{2,1,0:T(8,128)(2,1)S(1)}, u32[]{:S(2)}, u32[]{:S(2)}) %collective-permute-start.3) | collective-permute-done | bytes 131104 | tf_op jit(solution)/shard_map/ppermute | solution.py:11
  46.2 0.3 fusion.52
  47.3 7.8 %collective-permute-done.4 = bf16[32,16,128]{2,1,0:T(8,128)(2,1)S(1)} collective-permute-done((bf16[32,16,128]{2,1,0:T(8,128)(2,1)S(1)}, bf16[32,16,128]{2,1,0:T(8,128)(2,1)S(1)}, u32[]{:S(2)}, u32[]{:S(2)}) %collective-permute-start.4) | collective-permute-done | bytes 131104 | tf_op jit(solution)/shard_map/ppermute | solution.py:11
  55.3 0.3 fusion.60
  56.4 0.3 fusion.68
  57.6 0.3 fusion.76
  58.8 0.3 fusion.84
  59.7 0.6 copy-done.7
  60.8 0.7 %pad_maximum_fusion = f32[2,16,2048]{2,1,0:T(8,128)} fusion(f32[1,16,2048]{2,1,0:T(8,128)S(1)} %get-tuple-element.178, f32[1,16,2048]{2,1,0:T(8,128)S(1)} %get-tuple-element.177), kind=kLoop, calls=%fused_computation.97 | loop fusion | flops 65536 | bytes 524288 | tf_op jit(solution)/shard_map/stack | solution.py:111
  (107 shorter events, 12.1 us)
Async XLA Ops:
  0.0 3.3 %copy-start = (bf16[64,64]{1,0:T(8,128)(2,1)S(1)}, bf16[64,64]{1,0:T(8,128)(2,1)}, u32[]{:S(2)}) copy-start(bf16[64,64]{1,0:T(8,128)(2,1)} %param.12) | copy-start | bytes 24580
  0.0 2.0 %copy-start.1 = (f32[11,3,32,64]{3,2,1,0:T(8,128)S(1)}, f32[11,3,32,64]{3,2,1,0:T(8,128)}, u32[]{:S(2)}) copy-start(f32[11,3,32,64]{3,2,1,0:T(8,128)} %param.14) | copy-start | bytes 811012
  2.0 0.7 %copy-start.8 = (f32[2048]{0:T(1024)S(1)}, f32[2048]{0:T(1024)}, u32[]{:S(2)}) copy-start(f32[2048]{0:T(1024)} %param.11) | copy-start | bytes 24580
  2.0 0.9 %copy-start.3 = (f32[16,2048]{1,0:T(8,128)S(1)}, f32[16,2048]{1,0:T(8,128)}, u32[]{:S(2)}) copy-start(f32[16,2048]{1,0:T(8,128)} %param.10) | copy-start | bytes 393220
  3.8 1.0 %copy-start.2 = (bf16[11,2,64,64]{3,2,1,0:T(8,128)(2,1)S(1)}, bf16[11,2,64,64]{3,2,1,0:T(8,128)(2,1)}, u32[]{:S(2)}) copy-start(bf16[11,2,64,64]{3,2,1,0:T(8,128)(2,1)} %param.13) | copy-start | bytes 540676
  8.5 4.0 %copy-start.4 = (f32[2,32,64]{2,1,0:T(8,128)S(1)}, f32[2,32,64]{2,1,0:T(8,128)}, u32[]{:S(2)}) copy-start(f32[2,32,64]{2,1,0:T(8,128)} %param.16) | copy-start | bytes 49156
  8.5 6.5 %collective-permute-start = (bf16[32,16,128]{2,1,0:T(8,128)(2,1)S(1)}, bf16[32,16,128]{2,1,0:T(8,128)(2,1)S(1)}, u32[]{:S(2)}, u32[]{:S(2)}) collective-permute-start(bf16[32,16,128]{2,1,0:T(8,128)(2,1)S(1)} %get-tuple-element.14), channel_id=1, source_target_pairs={{0,8},{8,0},{16,24},{24,16},{1,9},{9,1},{17,25},{25,17},{2,10},{10... | collective-permute-start | bytes 393224 | tf_op jit(solution)/shard_map/ppermute | solution.py:11
  12.7 0.7 %copy-start.5 = (f32[32,64]{1,0:T(8,128)S(1)}, f32[32,64]{1,0:T(8,128)}, u32[]{:S(2)}) copy-start(f32[32,64]{1,0:T(8,128)} %param.17) | copy-start | bytes 24580
  15.9 5.0 %collective-permute-start.1 = (bf16[32,16,128]{2,1,0:T(8,128)(2,1)S(1)}, bf16[32,16,128]{2,1,0:T(8,128)(2,1)S(1)}, u32[]{:S(2)}, u32[]{:S(2)}) collective-permute-start(bf16[32,16,128]{2,1,0:T(8,128)(2,1)S(1)} %get-tuple-element.12), channel_id=1, source_target_pairs={{0,16},{8,24},{16,0},{24,8},{1,17},{9,25},{17,1},{25,9},{2,18},{10... | collective-permute-start | bytes 393224 | tf_op jit(solution)/shard_map/ppermute | solution.py:11
  22.4 6.3 %copy-start.9 = (f32[2048]{0:T(1024)S(1)}, f32[2048]{0:T(1024)}, u32[]{:S(2)}) copy-start(f32[2048]{0:T(1024)} %param.19) | copy-start | bytes 24580
  22.4 14.3 %all-to-all-start = ((bf16[32,16,128]{2,1,0:T(8,128)(2,1)}), bf16[32,16,128]{2,1,0:T(8,128)(2,1)S(1)}, u32[]{:S(2)}, u32[]{:S(2)}) async-start(bf16[32,16,128]{2,1,0:T(8,128)(2,1)} %pad_maximum_fusion.5), calls=%async_computation | async-start | bytes 262144 | tf_op jit(solution)/shard_map/all_to_all | solution.py:86
  36.7 0.7 %copy-start.6 = (bf16[64,64]{1,0:T(8,128)(2,1)S(1)}, bf16[64,64]{1,0:T(8,128)(2,1)}, u32[]{:S(2)}) copy-start(bf16[64,64]{1,0:T(8,128)(2,1)} %param.15) | copy-start | bytes 24580
  38.0 1.4 %collective-permute-start.2 = (bf16[32,16,128]{2,1,0:T(8,128)(2,1)S(1)}, bf16[32,16,128]{2,1,0:T(8,128)(2,1)S(1)}, u32[]{:S(2)}, u32[]{:S(2)}) collective-permute-start(bf16[32,16,128]{2,1,0:T(8,128)(2,1)S(1)} %get-tuple-element.10), channel_id=1, source_target_pairs={{0,1},{1,0},{2,3},{3,2},{4,5},{5,4},{6,7},{7,6},{8,9},{9,8},{10,11... | collective-permute-start | bytes 393224 | tf_op jit(solution)/shard_map/ppermute | solution.py:11
  40.2 5.8 %collective-permute-start.3 = (bf16[32,16,128]{2,1,0:T(8,128)(2,1)S(1)}, bf16[32,16,128]{2,1,0:T(8,128)(2,1)S(1)}, u32[]{:S(2)}, u32[]{:S(2)}) collective-permute-start(bf16[32,16,128]{2,1,0:T(8,128)(2,1)S(1)} %get-tuple-element.8), channel_id=1, source_target_pairs={{0,2},{1,3},{2,0},{3,1},{4,6},{5,7},{6,4},{7,5},{8,10},{9,11},{10,... | collective-permute-start | bytes 393224 | tf_op jit(solution)/shard_map/ppermute | solution.py:11
  46.8 8.2 %collective-permute-start.4 = (bf16[32,16,128]{2,1,0:T(8,128)(2,1)S(1)}, bf16[32,16,128]{2,1,0:T(8,128)(2,1)S(1)}, u32[]{:S(2)}, u32[]{:S(2)}) collective-permute-start(bf16[32,16,128]{2,1,0:T(8,128)(2,1)S(1)} %get-tuple-element.6), channel_id=1, source_target_pairs={{0,4},{1,5},{2,6},{3,7},{4,0},{5,1},{6,2},{7,3},{8,12},{9,13},{10,... | collective-permute-start | bytes 393224 | tf_op jit(solution)/shard_map/ppermute | solution.py:11
  59.5 0.7 %copy-start.7 = (bf16[64,64]{1,0:T(8,128)(2,1)S(1)}, bf16[64,64]{1,0:T(8,128)(2,1)}, u32[]{:S(2)}) copy-start(bf16[64,64]{1,0:T(8,128)(2,1)} %param.18) | copy-start | bytes 24580
where the time goes:
time: 62.1 us; the launch traced here: 61.5 us
  waiting for transfers between devices  25.3 us (41%)
  starting transfers between devices  12.3 us (20%)
  other arithmetic  10.1 us (16%)
  local copies, waits for them, and re-layouts  9.05 us (15%)
  matrix products  4.06 us (7%)
    ppermute x5, waiting for transfers between devices, swapped(): lax.ppermute(shard, axis, [(i, i ^ 1 << stride) for i in range(lax.axis_s...  18.2 us
    all_to_all x1, waiting for transfers between devices, shards(): lax.all_to_all(coeffs, ('src', 'tgt'), split_axis=0, concat_axis=0, tiled...  7.1 us
    another operation x35, other arithmetic  6.4 us
    all_to_all x1, starting transfers between devices, shards(): lax.all_to_all(coeffs, ('src', 'tgt'), split_axis=0, concat_axis=0, tiled...  6.27 us
    ppermute x5, starting transfers between devices, swapped(): lax.ppermute(shard, axis, [(i, i ^ 1 << stride) for i in range(lax.axis_s...  6.05 us
    cos x5, local copies, waits for them, and re-layouts, rotate(): cosine = jnp.cos(angles)[:, None, :]  3.61 us
    dot_general x11, matrix products, translate(): summed = jnp.dot(joined, weights, preferred_element_type=jnp.float32)  3.42 us
    unnamed x20, local copies, waits for them, and re-layouts  2.7 us
  transfers between devices with their start and end apart: 6, of which 6 were waited for; matrix products, arithmetic and copies ran while one was open for 5% of the time, Pallas kernels for 0%

commit v1 on v0

v1 whole, which is shorter than its diff:
```python
import functools

import jax
import jax.numpy as jnp
from jax import lax
from jax.experimental import pallas as pl
from jax.experimental.pallas import tpu as pltpu
from jax.sharding import PartitionSpec as P

LOCAL_SRC = 3
LOCAL_TGT = 3
MESH = pl.DeviceIdType.MESH
F32 = jnp.float32
BF16 = jnp.bfloat16

PI_HI = 3.140625
PI_LO = 9.67653589793e-4
SIN_C = (2.605166276178326e-06, -0.00019809046357444052, 0.008333050617328575, -0.16666657969904702, 0.9999999957158396)
COS_C = (-2.605107617861078e-07, 2.4760135505794177e-05, -0.0013888360842290288, 0.04166663620890442, -0.49999999356955516, 0.9999999997799034)


def cos_sin(x):
    k = lax.round(x * (1.0 / 3.141592653589793), lax.RoundingMethod.TO_NEAREST_EVEN)
    r = (x - k * PI_HI) - k * PI_LO
    z = r * r
    c = jnp.full_like(z, COS_C[0])
    for a in COS_C[1:]:
        c = c * z + a
    s = jnp.full_like(z, SIN_C[0])
    for a in SIN_C[1:]:
        s = s * z + a
    s = s * r
    half = k * 0.5
    odd = jnp.abs(half - lax.round(half, lax.RoundingMethod.TO_NEAREST_EVEN))
    sign = 1.0 - 4.0 * odd
    return c * sign, s * sign


def lane_low(shape, half):
    return lax.broadcasted_iota(jnp.int32, shape, len(shape) - 1) < half


def dup(x):
    return jnp.concatenate([x, x], -1)


def dup_halves(x, half):
    y = pltpu.roll(x, half, x.ndim - 1)
    low = lane_low(x.shape, half)
    return jnp.where(low, x, y), jnp.where(low, y, x)


def xor_rows(x, h):
    rows = x.shape[0]
    up = pltpu.roll(x, rows - h, 0)
    down = pltpu.roll(x, h, 0)
    row = lax.broadcasted_iota(jnp.int32, x.shape, 0)
    return jnp.where((row // h) % 2 == 0, up, down)


def xor_lead(x, h):
    return jnp.concatenate([x[i ^ h : (i ^ h) + 1] for i in range(x.shape[0])], 0)


def kernel(
    S, T, levels, src_bits, tgt_bits,
    values, sphase, leaf, lint, lphase, mint, mphase, fphase, fint, tphase,
    out,
    w, wl, wm, wf, tc, ts, ph_src, pk2, pk, ph_tgt, send1, recv1, xa, xb, send2, recv2,
    ps_send, ps_recv, pt_send, pt_recv, c1_send, c1_recv, c2_send, c2_recv,
):
    s_me = lax.axis_index("src")
    t_me = lax.axis_index("tgt")
    half = leaf.shape[1]
    R = S * T
    rhs = values.shape[0]
    rows = T * rhs
    K = LOCAL_SRC + src_bits
    M = K + tgt_bits
    N = levels

    barrier = pltpu.get_barrier_semaphore()
    for j in range(1, S):
        pl.semaphore_signal(barrier, inc=1, device_id=(lax.rem(s_me + j, S), t_me), device_id_type=MESH)
    for j in range(1, T):
        pl.semaphore_signal(barrier, inc=1, device_id=(s_me, lax.rem(t_me + j, T)), device_id_type=MESH)

    def arr(q):
        if q < 2:
            return mphase[q]
        return lphase[K + (q - 2) // 3, (q - 2) % 3]

    nq = 2 + 3 * tgt_bits
    Q = (nq + 1) // 2
    RP = pk.shape[0] // T
    for q in range(Q):
        a = arr(2 * q)
        b = arr(2 * q + 1) if 2 * q + 1 < nq else a
        pk2[q * R : (q + 1) * R, :] = jnp.concatenate([a, b], -1)
    for d in range(T):
        pk[d * RP : d * RP + Q * S, :] = pk2[pl.ds(d, Q * S, stride=T), :]

    sgn = jnp.where(lane_low((R, 2 * half), half), -1.0, 1.0)

    def put(idx, angle):
        c, s = cos_sin(angle * sgn)
        tc[idx] = c
        ts[idx] = s

    def put_level(n, prev, own, other, h):
        oth = xor_rows(other, h)
        put(2 * n, own if prev is None else prev + own)
        put(2 * n + 1, oth if prev is None else prev + oth)

    def lp(n, q):
        return dup(lphase[n, q])

    I_SEND1, I_MID, I_SEND2, I_FIN, I_TGT, I_SRC = (2 * N + i for i in range(6))

    low16 = lane_low((sphase.shape[0], 2 * half), half)

    def point_rows(ref):
        lo, hi = dup_halves(ref[...], half)
        n = lo.shape[0]
        return jnp.concatenate([jnp.concatenate([lo[i : i + 1], hi[i : i + 1]], 0) for i in range(n)], 0)

    c, s = cos_sin(point_rows(sphase))
    tc[I_SRC] = jnp.where(lane_low(c.shape, half), c, -s)
    for n in range(LOCAL_SRC):
        put_level(n, None if n == 0 else lp(n - 1, 2), lp(n, 0), lp(n, 1), 2**n)
    put(I_SEND1, lp(LOCAL_SRC - 1, 2))

    def fill(dst, r, L):
        z = jnp.zeros_like(L)
        lz = jnp.concatenate([L, z], 1)
        zl = jnp.concatenate([z, L], 1)
        wd = 2 * half
        dst[r : r + half, 0:wd] = lz
        dst[r : r + half, wd : 2 * wd] = zl
        dst[r + half : r + wd, 0:wd] = zl
        dst[r + half : r + wd, wd : 2 * wd] = lz

    fill(wl, 0, leaf[...])
    for n in range(LOCAL_SRC):
        fill(w.at[n], 0, lint[n, 0])
        fill(w.at[n], 2 * half, lint[n, 1])

    pl.semaphore_wait(barrier, S - 1 + T - 1)

    def blk(i):
        return pl.ds(pl.multiple_of(i * T, T), T)

    def ps_copy(j):
        e = lax.rem(s_me + j, S)
        return pltpu.make_async_remote_copy(
            src_ref=lphase.at[pl.ds(LOCAL_SRC, src_bits), :, blk(e), :],
            dst_ref=ph_src.at[:, :, blk(s_me), :],
            send_sem=ps_send.at[j], recv_sem=ps_recv.at[j],
            device_id=(e, t_me), device_id_type=MESH,
        )

    def pt_copy(j):
        e = lax.rem(t_me + j, T)
        return pltpu.make_async_remote_copy(
            src_ref=pk.at[pl.ds(pl.multiple_of(e * RP, 8), RP), :],
            dst_ref=ph_tgt.at[pl.ds(pl.multiple_of(t_me * RP, 8), RP), :],
            send_sem=pt_send.at[j], recv_sem=pt_recv.at[j],
            device_id=(s_me, e), device_id_type=MESH,
        )

    for j in range(1, S):
        ps_copy(j).start()
    for j in range(1, T):
        pt_copy(j).start()

    def tab(idx, i):
        return tc[idx, blk(i), :][:, None, :], ts[idx, blk(i), :][:, None, :]

    wd = 2 * half

    def split(y):
        y = y.reshape(T, rhs, 2 * wd)
        return y[:, :, :wd], y[:, :, wd:]

    def rot(v, sw, idx, i):
        c, s = tab(idx, i)
        return v * c + sw * s

    def dot(x, m):
        return jnp.dot(x, m, preferred_element_type=F32)

    def step(v, sw, n, i, h):
        own = rot(v, sw, 2 * n, i).astype(BF16)
        oth = xor_lead(rot(v, sw, 2 * n + 1, i), h).astype(BF16)
        x = jnp.concatenate([own, oth], -1).reshape(rows, 2 * wd)
        return split(dot(x, w[n]))

    def c1_copy(j):
        e = lax.rem(s_me + j, S)
        return pltpu.make_async_remote_copy(
            src_ref=send1.at[e], dst_ref=recv1.at[s_me],
            send_sem=c1_send.at[j], recv_sem=c1_recv.at[j],
            device_id=(e, t_me), device_id_type=MESH,
        )

    for j in range(1, S + 1):
        e = lax.rem(s_me + j, S)
        span = T * half
        vals = values[:, pl.ds(pl.multiple_of(e * span, span), span)]
        parts = []
        for p in range(T // 2):
            parts.extend(dup_halves(vals[:, p * wd : (p + 1) * wd], half))
        x = jnp.stack(parts, 0) * tc[I_SRC, blk(e), :][:, None, :]
        v, sw = split(dot(x.astype(BF16).reshape(rows, wd), wl[...]))
        for n in range(LOCAL_SRC):
            v, sw = step(v, sw, n, e, 2**n)
        res = rot(v, sw, I_SEND1, e).astype(BF16)
        if j < S:
            send1[e] = res
            c1_copy(j).start()
        else:
            recv1[s_me] = res

    for n in range(LOCAL_SRC, N):
        fill(w.at[n], 0, lint[n, 0])
        fill(w.at[n], 2 * half, lint[n, 1])
    fill(wm, 0, mint[...])
    fill(wf, 0, fint[...])

    ph_src[:, :, blk(s_me), :] = lphase[LOCAL_SRC:K, :, blk(s_me), :]
    own_rows = pl.ds(pl.multiple_of(t_me * RP, 8), RP)
    ph_tgt[own_rows, :] = pk[own_rows, :]

    for n in range(M, N):
        put_level(n, None if n == M else lp(n - 1, 2), lp(n, 0), lp(n, 1), 2 ** (n - M))
    put(I_FIN, lp(N - 1, 2) + dup(fphase[...]))
    put(I_TGT, point_rows(tphase))

    for j in range(1, S):
        ps_copy(j).wait()
    for b in range(src_bits):
        n = LOCAL_SRC + b
        prev = None if b == 0 else dup(ph_src[b - 1, 2])
        put_level(n, prev, dup(ph_src[b, 0]), dup(ph_src[b, 1]), T * 2**b)

    for j in range(1, T):
        pt_copy(j).wait()
    ang = []
    for q in range(Q):
        packed = jnp.concatenate(
            [ph_tgt[pl.ds(q * S + i, T, stride=RP), :] for i in range(S)], 0
        )
        ang.extend(dup_halves(packed, half))
    put(I_MID, dup(ph_src[src_bits - 1, 2]) + ang[0])
    for b in range(tgt_bits):
        n = K + b
        prev = ang[1] if b == 0 else ang[2 + 3 * (b - 1) + 2]
        put_level(n, prev, ang[2 + 3 * b], ang[2 + 3 * b + 1], 2**b)
    put(I_SEND2, ang[2 + 3 * (tgt_bits - 1) + 2])

    for j in range(1, S):
        c1_copy(j).wait()

    bufs = (xa, xb)
    for b in range(src_bits):
        n = LOCAL_SRC + b
        dst = bufs[b % 2]
        for i in range(S):
            if b == 0:
                v = recv1[i].astype(F32)
                sw = pltpu.roll(v, half, 2)
            else:
                v, sw = split(dot(bufs[(b - 1) % 2][i], w[n - 1]))
            own = rot(v, sw, 2 * n, i).astype(BF16)
            oth = rot(v, sw, 2 * n + 1, i).astype(BF16)
            dst[i, :, :wd] = own.reshape(rows, wd)
            dst[i ^ 2**b, :, wd:] = oth.reshape(rows, wd)

    def c2_copy(i, j):
        e = lax.rem(t_me + j, T)
        return pltpu.make_async_remote_copy(
            src_ref=send2.at[i, e], dst_ref=recv2.at[i, t_me],
            send_sem=c2_send.at[i, j], recv_sem=c2_recv.at[i, j],
            device_id=(s_me, e), device_id_type=MESH,
        )

    for i in range(S):
        v, sw = split(dot(bufs[(src_bits - 1) % 2][i], w[K - 1]))
        x = rot(v, sw, I_MID, i).astype(BF16).reshape(rows, wd)
        v, sw = split(dot(x, wm[...]))
        for b in range(tgt_bits):
            v, sw = step(v, sw, K + b, i, 2**b)
        send2[i] = rot(v, sw, I_SEND2, i).astype(BF16)
        for j in range(1, T):
            c2_copy(i, j).start()
        recv2[i, t_me] = send2[i, t_me]

    low3 = lane_low((rhs, wd), half)
    for i in range(S):
        for j in range(1, T):
            c2_copy(i, j).wait()
        v = recv2[i].astype(F32)
        sw = pltpu.roll(v, half, 2)
        for n in range(M, N):
            v, sw = step(v, sw, n, i, 2 ** (n - M))
        x = rot(v, sw, I_FIN, i).astype(BF16).reshape(rows, wd)
        v, sw = split(dot(x, wf[...]))
        r = rot(v, sw, I_TGT, i)
        rr = pltpu.roll(r, half, 2)
        for p in range(T // 2):
            col = pl.ds(i * T * half + p * wd, wd)
            out[0, :, col] = jnp.where(low3, r[2 * p], rr[2 * p + 1])
            out[1, :, col] = jnp.where(low3, rr[2 * p], r[2 * p + 1])


def shards(
    source_values, source_phase, leaf_interp, level_interp, level_phase,
    middle_interp, middle_phase, final_phase, final_interp, target_phase,
):
    S = lax.axis_size("src")
    T = lax.axis_size("tgt")
    R = level_phase.shape[2]
    assert R == S * T
    rhs = source_values.shape[0]
    half = leaf_interp.shape[1]
    wd = 2 * half
    N = level_phase.shape[0]
    src_bits = S.bit_length() - 1
    tgt_bits = T.bit_length() - 1
    assert N == LOCAL_SRC + src_bits + tgt_bits + LOCAL_TGT
    Q = (2 + 3 * tgt_bits + 1) // 2
    RP = -(-Q * S // 8) * 8
    ntab = 2 * N + 6
    vm = pltpu.VMEM
    dma = pltpu.SemaphoreType.DMA
    return pl.pallas_call(
        functools.partial(kernel, S, T, N, src_bits, tgt_bits),
        out_shape=jax.ShapeDtypeStruct((2,) + source_values.shape, F32),
        in_specs=[pl.BlockSpec(memory_space=pltpu.VMEM)] * 10,
        out_specs=pl.BlockSpec(memory_space=pltpu.VMEM),
        scratch_shapes=[
            vm((N, 2 * wd, 2 * wd), BF16), vm((wd, 2 * wd), BF16),
            vm((wd, 2 * wd), BF16), vm((wd, 2 * wd), BF16),
            vm((ntab, R, wd), F32), vm((ntab, R, wd), F32),
            vm((src_bits, 3, R, half), F32), vm((Q * R, wd), F32),
            vm((T * RP, wd), F32), vm((T * RP, wd), F32),
            vm((S, T, rhs, wd), BF16), vm((S, T, rhs, wd), BF16),
            vm((S, T * rhs, 2 * wd), BF16), vm((S, T * rhs, 2 * wd), BF16),
            vm((S, T, rhs, wd), BF16), vm((S, T, rhs, wd), BF16),
            dma((S,)), dma((S,)), dma((T,)), dma((T,)),
            dma((S,)), dma((S,)), dma((S, T)), dma((S, T)),
        ],
        compiler_params=pltpu.CompilerParams(collective_id=0, has_side_effects=True),
    )(
        source_values, source_phase.reshape(-1, wd), leaf_interp, level_interp, level_phase,
        middle_interp, middle_phase, final_phase, final_interp, target_phase.reshape(-1, wd),
    )


def solution(mesh):
    return jax.shard_map(
        shards,
        mesh=mesh,
        in_specs=(
            P(None, ("src", "tgt")),
            P(("src", "tgt")),
            P(),
            P(),
            P(None, None, ("src", "tgt"), None),
            P(),
            P(None, ("src", "tgt"), None),
            P(("src", "tgt"), None),
            P(),
            P(("src", "tgt")),
        ),
        out_specs=P(None, None, ("src", "tgt")),
        check_vma=False,
    )
```

time: 62.1 us -> 22 us (0.35)
  waiting for transfers between devices: 25.3 us -> 0 us
  Pallas kernels: 0 us -> 20.1 us
  starting transfers between devices: 12.3 us -> 0 us
  other arithmetic: 10.1 us -> 0 us
  local copies, waits for them, and re-layouts: 9.05 us -> 1.67 us
  matrix products: 4.06 us -> 0 us
    pallas_call x0 -> x1, Pallas kernels: none -> 20.1 us  [shards(): pl.pallas_call(functools.partial(kernel, S, T, N, src_bits, tgt_bits), ou...]
    ppermute x5 -> x0, waiting for transfers between devices: 18.2 us -> none  [swapped(): lax.ppermute(shard, axis, [(i, i ^ 1 << stride) for i in range(lax.axis_s...]
    another operation x36 -> x0, other arithmetic: 7.12 us -> none
    all_to_all x1 -> x0, waiting for transfers between devices: 7.1 us -> none  [shards(): lax.all_to_all(coeffs, ('src', 'tgt'), split_axis=0, concat_axis=0, tiled...]
    all_to_all x1 -> x0, starting transfers between devices: 6.27 us -> none  [shards(): lax.all_to_all(coeffs, ('src', 'tgt'), split_axis=0, concat_axis=0, tiled...]
    ppermute x5 -> x0, starting transfers between devices: 6.05 us -> none  [swapped(): lax.ppermute(shard, axis, [(i, i ^ 1 << stride) for i in range(lax.axis_s...]
    dot_general x14 -> x0, matrix products: 4.06 us -> none  [the longest x11 3.42 us: translate(): summed = jnp.dot(joined, weights, preferred_element_type=jnp.float32)]
    cos x7 -> x0, local copies, waits for them, and re-layouts: 3.71 us -> none  [the longest x5 3.61 us: rotate(): cosine = jnp.cos(angles)[:, None, :]]
  transfers between devices with their start and end apart: 6 -> 0, of which waited for: 6 -> 0; matrix products, arithmetic and copies ran while one was open for 5% -> 0% of each run, Pallas kernels for 0% -> 0%
where the time goes in v1:
time: 22 us; the launch traced here: 21.8 us
  Pallas kernels  20.1 us (91%)
  local copies, waits for them, and re-layouts  1.67 us (8%)
    pallas_call x1, Pallas kernels, shards(): pl.pallas_call(functools.partial(kernel, S, T, N, src_bits, tgt_bits), ou...  20.1 us
    unnamed x1, local copies, waits for them, and re-layouts  1.67 us

profile of v1, /device:TPU:0, one launch (start us, length us, event | category | flops | bytes accessed | tf_op | source)
XLA Modules:
  0.0 21.8 jit_solution(686928827369478809)
XLA Ops:
  0.0 20.1 %shard_map.100 = f32[2,16,2048]{2,1,0:T(8,128)} custom-call(f32[16,2048]{1,0:T(8,128)} %values.1, f32[16,128]{1,0:T(8,128)} %bitcast.2, bf16[64,64]{1,0:T(8,128)(2,1)} %leaf.1, bf16[11,2,64,64]{3,2,1,0:T(8,128)(2,1)} %lint.1, f32[11,3,32,64]{3,2,1,0:T(8,128)} %lphase.1, bf16[64,64]{1,0:T(8,128)(2,1)} %mint.1, f32[2,32,64]{2,1,0:T(8,128)} %mphase.1, ...), custom_call_target="tpu_custom_call" | custom-call | tf_op jit(solution)/shard_map/pallas_call | solution.py:336
  20.1 1.7 %copy.12 = f32[2,16,2048]{2,1,0:T(8,128)} copy(f32[2,16,2048]{2,1,0:T(8,128)} %shard_map.100) | data formatting | bytes 524288

commit v2 on v1

v2 whole, which is shorter than its diff:
```python
import functools

import jax
import jax.numpy as jnp
from jax import lax
from jax.experimental import pallas as pl
from jax.experimental.pallas import tpu as pltpu
from jax.sharding import PartitionSpec as P

LOCAL_SRC = 3
LOCAL_TGT = 3
MESH = pl.DeviceIdType.MESH
GROUP = 2
VLIM = 67043328
F32 = jnp.float32
BF16 = jnp.bfloat16

PI_HI = 3.140625
PI_LO = 9.67653589793e-4
SIN_C = (2.605166276178326e-06, -0.00019809046357444052, 0.008333050617328575, -0.16666657969904702, 0.9999999957158396)
COS_C = (-2.605107617861078e-07, 2.4760135505794177e-05, -0.0013888360842290288, 0.04166663620890442, -0.49999999356955516, 0.9999999997799034)


def cos_sin(x):
    k = lax.round(x * (1.0 / 3.141592653589793), lax.RoundingMethod.TO_NEAREST_EVEN)
    r = (x - k * PI_HI) - k * PI_LO
    z = r * r
    c = jnp.full_like(z, COS_C[0])
    for a in COS_C[1:]:
        c = c * z + a
    s = jnp.full_like(z, SIN_C[0])
    for a in SIN_C[1:]:
        s = s * z + a
    s = s * r
    half = k * 0.5
    odd = jnp.abs(half - lax.round(half, lax.RoundingMethod.TO_NEAREST_EVEN))
    sign = 1.0 - 4.0 * odd
    return c * sign, s * sign


def lane_low(shape, half):
    return lax.broadcasted_iota(jnp.int32, shape, len(shape) - 1) < half


def dup(x):
    return jnp.concatenate([x, x], -1)


def dup_halves(x, half):
    y = pltpu.roll(x, half, x.ndim - 1)
    low = lane_low(x.shape, half)
    return jnp.where(low, x, y), jnp.where(low, y, x)


def xor_rows(x, h):
    rows = x.shape[0]
    up = pltpu.roll(x, rows - h, 0)
    down = pltpu.roll(x, h, 0)
    row = lax.broadcasted_iota(jnp.int32, x.shape, 0)
    return jnp.where((row // h) % 2 == 0, up, down)


def xor_lead(x, h):
    return jnp.concatenate([x[i ^ h : (i ^ h) + 1] for i in range(x.shape[0])], 0)


def xor_index(i, j, size):
    bit = 1
    res = i
    while bit < size:
        if j & bit:
            res = res + bit * (1 - 2 * lax.rem(i // bit, 2))
        bit *= 2
    return res


def kernel(
    S, T, levels, src_bits, tgt_bits,
    values_h, sphase_h, leaf_h, lint_h, lphase_h, mint_h, mphase_h, fphase_h, fint_h, tphase_h,
    out,
    values, sphase, leaf, lint, lphase, mint, mphase, fphase, fint, tphase, obuf, in_sem, out_sem,
    w, wl, wm, wf, tc, ts, ph_src, pk2, pk, ph_tgt, send1, recv1, xa, xb, send2, recv2,
    ps_send, ps_recv, pt_send, pt_recv, c1_send, c1_recv, c2_send, c2_recv,
):
    s_me = lax.axis_index("src")
    t_me = lax.axis_index("tgt")
    half = leaf.shape[1]
    span = T * half
    R = S * T
    rhs = values.shape[0]
    rows = T * rhs
    K = LOCAL_SRC + src_bits
    M = K + tgt_bits
    N = levels

    barrier = pltpu.get_barrier_semaphore()
    for j in range(1, S):
        pl.semaphore_signal(barrier, inc=1, device_id=(lax.rem(s_me + j, S), t_me), device_id_type=MESH)
    for j in range(1, T):
        pl.semaphore_signal(barrier, inc=1, device_id=(s_me, lax.rem(t_me + j, T)), device_id_type=MESH)

    loads = [
        pltpu.make_async_copy(a, b, in_sem.at[i])
        for i, (a, b) in enumerate(
            (
                (sphase_h, sphase), (lphase_h, lphase), (leaf_h, leaf), (values_h, values),
                (lint_h, lint), (mphase_h, mphase), (fphase_h, fphase), (tphase_h, tphase),
                (mint_h, mint), (fint_h, fint),
            )
        )
    ]
    for load in loads:
        load.start()
    for load in loads[:3]:
        load.wait()

    sgn = jnp.where(lane_low((R, 2 * half), half), -1.0, 1.0)

    def put(idx, angle):
        c, s = cos_sin(angle * sgn)
        tc[idx] = c
        ts[idx] = s

    def put_level(n, prev, own, other, h):
        oth = xor_rows(other, h)
        put(2 * n, own if prev is None else prev + own)
        put(2 * n + 1, oth if prev is None else prev + oth)

    def lp(n, q):
        return dup(lphase[n, q])

    I_SEND1, I_MID, I_SEND2, I_FIN, I_TGT, I_SRC = (2 * N + i for i in range(6))

    low16 = lane_low((sphase.shape[0], 2 * half), half)

    def point_rows(ref):
        lo, hi = dup_halves(ref[...], half)
        n = lo.shape[0]
        return jnp.concatenate([jnp.concatenate([lo[i : i + 1], hi[i : i + 1]], 0) for i in range(n)], 0)

    c, s = cos_sin(point_rows(sphase))
    tc[I_SRC] = jnp.where(lane_low(c.shape, half), c, -s)
    for n in range(LOCAL_SRC):
        put_level(n, None if n == 0 else lp(n - 1, 2), lp(n, 0), lp(n, 1), 2**n)
    put(I_SEND1, lp(LOCAL_SRC - 1, 2))

    def fill(dst, r, L):
        z = jnp.zeros_like(L)
        lz = jnp.concatenate([L, z], 1)
        zl = jnp.concatenate([z, L], 1)
        wd = 2 * half
        dst[r : r + half, 0:wd] = lz
        dst[r : r + half, wd : 2 * wd] = zl
        dst[r + half : r + wd, 0:wd] = zl
        dst[r + half : r + wd, wd : 2 * wd] = lz

    fill(wl, 0, leaf[...])
    loads[4].wait()
    for n in range(LOCAL_SRC):
        fill(w.at[n], 0, lint[n, 0])
        fill(w.at[n], 2 * half, lint[n, 1])

    def blk(i):
        return pl.ds(pl.multiple_of(i * T, T), T)

    def ps_copy(j):
        e = xor_index(s_me, j, S)
        return pltpu.make_async_remote_copy(
            src_ref=lphase.at[pl.ds(LOCAL_SRC, src_bits), :, blk(e), :],
            dst_ref=ph_src.at[:, :, blk(s_me), :],
            send_sem=ps_send.at[j], recv_sem=ps_recv.at[j],
            device_id=(e, t_me), device_id_type=MESH,
        )

    def pt_copy(j):
        e = xor_index(t_me, j, T)
        return pltpu.make_async_remote_copy(
            src_ref=pk.at[pl.ds(pl.multiple_of(e * RP, 8), RP), :],
            dst_ref=ph_tgt.at[pl.ds(pl.multiple_of(t_me * RP, 8), RP), :],
            send_sem=pt_send.at[j], recv_sem=pt_recv.at[j],
            device_id=(s_me, e), device_id_type=MESH,
        )

    def tab(idx, i):
        return tc[idx, blk(i), :][:, None, :], ts[idx, blk(i), :][:, None, :]

    wd = 2 * half

    def split(y):
        y = y.reshape(T, rhs, 2 * wd)
        return y[:, :, :wd], y[:, :, wd:]

    def rot(v, sw, idx, i):
        c, s = tab(idx, i)
        return v * c + sw * s

    def dot(x, m):
        return jnp.dot(x, m, preferred_element_type=F32)

    def step(v, sw, n, i, h):
        own = rot(v, sw, 2 * n, i).astype(BF16)
        oth = xor_lead(rot(v, sw, 2 * n + 1, i), h).astype(BF16)
        x = jnp.concatenate([own, oth], -1).reshape(rows, 2 * wd)
        return split(dot(x, w[n]))

    def c1_copy(j):
        e = xor_index(s_me, j, S)
        return pltpu.make_async_remote_copy(
            src_ref=send1.at[e], dst_ref=recv1.at[s_me],
            send_sem=c1_send.at[j], recv_sem=c1_recv.at[j],
            device_id=(e, t_me), device_id_type=MESH,
        )

    loads[3].wait()
    state = []
    for e in range(S):
        parts = []
        for p in range(T // 2):
            parts.extend(dup_halves(values[:, e * span + p * wd : e * span + (p + 1) * wd], half))
        x = jnp.stack(parts, 0) * tc[I_SRC, blk(e), :][:, None, :]
        state.append(split(dot(x.astype(BF16).reshape(rows, wd), wl[...])))
    for n in range(LOCAL_SRC):
        state = [step(v, sw, n, e, 2**n) for e, (v, sw) in enumerate(state)]
    for e, (v, sw) in enumerate(state):
        send1[e] = rot(v, sw, I_SEND1, e).astype(BF16)

    loads[5].wait()
    def arr(q):
        if q < 2:
            return mphase[q]
        return lphase[K + (q - 2) // 3, (q - 2) % 3]

    nq = 2 + 3 * tgt_bits
    Q = (nq + 1) // 2
    RP = pk.shape[0] // T
    for q in range(Q):
        a = arr(2 * q)
        b = arr(2 * q + 1) if 2 * q + 1 < nq else a
        pk2[q * R : (q + 1) * R, :] = jnp.concatenate([a, b], -1)
    for d in range(T):
        pk[d * RP : d * RP + Q * S, :] = pk2[pl.ds(d, Q * S, stride=T), :]

    pl.semaphore_wait(barrier, S - 1 + T - 1)
    for j in range(S - 1, 0, -1):
        ps_copy(j).start()
    for j in range(T - 1, 0, -1):
        pt_copy(j).start()

    for j in range(S - 1, 0, -1):
        c1_copy(j).start()
    recv1[s_me] = send1[s_me]

    for load in loads[6:]:
        load.wait()
    for n in range(LOCAL_SRC, N):
        fill(w.at[n], 0, lint[n, 0])
        fill(w.at[n], 2 * half, lint[n, 1])
    fill(wm, 0, mint[...])
    fill(wf, 0, fint[...])

    ph_src[:, :, blk(s_me), :] = lphase[LOCAL_SRC:K, :, blk(s_me), :]
    own_rows = pl.ds(pl.multiple_of(t_me * RP, 8), RP)
    ph_tgt[own_rows, :] = pk[own_rows, :]

    for n in range(M, N):
        put_level(n, None if n == M else lp(n - 1, 2), lp(n, 0), lp(n, 1), 2 ** (n - M))
    put(I_FIN, lp(N - 1, 2) + dup(fphase[...]))
    put(I_TGT, point_rows(tphase))

    for j in range(1, S):
        ps_copy(j).wait()
    for b in range(src_bits):
        n = LOCAL_SRC + b
        prev = None if b == 0 else dup(ph_src[b - 1, 2])
        put_level(n, prev, dup(ph_src[b, 0]), dup(ph_src[b, 1]), T * 2**b)

    for j in range(1, T):
        pt_copy(j).wait()
    ang = []
    for q in range(Q):
        packed = jnp.concatenate(
            [ph_tgt[pl.ds(q * S + i, T, stride=RP), :] for i in range(S)], 0
        )
        ang.extend(dup_halves(packed, half))
    put(I_MID, dup(ph_src[src_bits - 1, 2]) + ang[0])
    for b in range(tgt_bits):
        n = K + b
        prev = ang[1] if b == 0 else ang[2 + 3 * (b - 1) + 2]
        put_level(n, prev, ang[2 + 3 * b], ang[2 + 3 * b + 1], 2**b)
    put(I_SEND2, ang[2 + 3 * (tgt_bits - 1) + 2])

    for j in range(1, S):
        c1_copy(j).wait()

    bufs = (xa, xb)
    for b in range(src_bits):
        n = LOCAL_SRC + b
        dst = bufs[b % 2]
        for i in range(S):
            if b == 0:
                v = recv1[i].astype(F32)
                sw = pltpu.roll(v, half, 2)
            else:
                v, sw = split(dot(bufs[(b - 1) % 2][i], w[n - 1]))
            own = rot(v, sw, 2 * n, i).astype(BF16)
            oth = rot(v, sw, 2 * n + 1, i).astype(BF16)
            dst[i, :, :wd] = own.reshape(rows, wd)
            dst[i ^ 2**b, :, wd:] = oth.reshape(rows, wd)

    def c2_copy(i, j):
        e = xor_index(t_me, j, T)
        return pltpu.make_async_remote_copy(
            src_ref=send2.at[i, e], dst_ref=recv2.at[i, t_me],
            send_sem=c2_send.at[i, j], recv_sem=c2_recv.at[i, j],
            device_id=(s_me, e), device_id_type=MESH,
        )

    for g in range(0, S, GROUP):
        blocks = range(g, min(g + GROUP, S))
        state = [split(dot(bufs[(src_bits - 1) % 2][i], w[K - 1])) for i in blocks]
        state = [rot(v, sw, I_MID, i).astype(BF16).reshape(rows, wd) for i, (v, sw) in zip(blocks, state)]
        state = [split(dot(x, wm[...])) for x in state]
        for b in range(tgt_bits):
            state = [step(v, sw, K + b, i, 2**b) for i, (v, sw) in zip(blocks, state)]
        for i, (v, sw) in zip(blocks, state):
            send2[i] = rot(v, sw, I_SEND2, i).astype(BF16)
        for i in blocks:
            for j in range(T - 1, 0, -1):
                c2_copy(i, j).start()
            recv2[i, t_me] = send2[i, t_me]

    low3 = lane_low((rhs, wd), half)

    def o_copy(i):
        cols = pl.ds(i * span, span)
        return pltpu.make_async_copy(obuf.at[:, :, cols], out.at[:, :, cols], out_sem.at[i])

    for g in range(0, S, GROUP):
        blocks = range(g, min(g + GROUP, S))
        for i in blocks:
            for j in range(1, T):
                c2_copy(i, j).wait()
        state = []
        for i in blocks:
            v = recv2[i].astype(F32)
            state.append((v, pltpu.roll(v, half, 2)))
        for n in range(M, N):
            state = [step(v, sw, n, i, 2 ** (n - M)) for i, (v, sw) in zip(blocks, state)]
        state = [rot(v, sw, I_FIN, i).astype(BF16).reshape(rows, wd) for i, (v, sw) in zip(blocks, state)]
        state = [split(dot(x, wf[...])) for x in state]
        for i, (v, sw) in zip(blocks, state):
            r = rot(v, sw, I_TGT, i)
            rr = pltpu.roll(r, half, 2)
            for p in range(T // 2):
                col = pl.ds(i * T * half + p * wd, wd)
                obuf[0, :, col] = jnp.where(low3, r[2 * p], rr[2 * p + 1])
                obuf[1, :, col] = jnp.where(low3, rr[2 * p], r[2 * p + 1])
            o_copy(i).start()
    for i in range(S):
        o_copy(i).wait()


def shards(
    source_values, source_phase, leaf_interp, level_interp, level_phase,
    middle_interp, middle_phase, final_phase, final_interp, target_phase,
):
    S = lax.axis_size("src")
    T = lax.axis_size("tgt")
    R = level_phase.shape[2]
    assert R == S * T
    rhs = source_values.shape[0]
    half = leaf_interp.shape[1]
    wd = 2 * half
    N = level_phase.shape[0]
    src_bits = S.bit_length() - 1
    tgt_bits = T.bit_length() - 1
    assert N == LOCAL_SRC + src_bits + tgt_bits + LOCAL_TGT
    Q = (2 + 3 * tgt_bits + 1) // 2
    RP = -(-Q * S // 8) * 8
    ntab = 2 * N + 6
    vm = pltpu.VMEM
    dma = pltpu.SemaphoreType.DMA
    args = (
        source_values, source_phase.reshape(-1, wd), leaf_interp, level_interp, level_phase,
        middle_interp, middle_phase, final_phase, final_interp, target_phase.reshape(-1, wd),
    )
    return pl.pallas_call(
        functools.partial(kernel, S, T, N, src_bits, tgt_bits),
        out_shape=jax.ShapeDtypeStruct((2,) + source_values.shape, F32),
        in_specs=[pl.BlockSpec(memory_space=pltpu.HBM)] * 10,
        out_specs=pl.BlockSpec(memory_space=pl.ANY),
        scratch_shapes=[vm(a.shape, a.dtype) for a in args] + [
            vm((2,) + source_values.shape, F32), dma((10,)), dma((S,)),
            vm((N, 2 * wd, 2 * wd), BF16), vm((wd, 2 * wd), BF16),
            vm((wd, 2 * wd), BF16), vm((wd, 2 * wd), BF16),
            vm((ntab, R, wd), F32), vm((ntab, R, wd), F32),
            vm((src_bits, 3, R, half), F32), vm((Q * R, wd), F32),
            vm((T * RP, wd), F32), vm((T * RP, wd), F32),
            vm((S, T, rhs, wd), BF16), vm((S, T, rhs, wd), BF16),
            vm((S, T * rhs, 2 * wd), BF16), vm((S, T * rhs, 2 * wd), BF16),
            vm((S, T, rhs, wd), BF16), vm((S, T, rhs, wd), BF16),
            dma((S,)), dma((S,)), dma((T,)), dma((T,)),
            dma((S,)), dma((S,)), dma((S, T)), dma((S, T)),
        ],
        compiler_params=pltpu.CompilerParams(
            collective_id=0, has_side_effects=True, vmem_limit_bytes=VLIM
        ),
    )(*args)


def solution(mesh):
    return jax.shard_map(
        shards,
        mesh=mesh,
        in_specs=(
            P(None, ("src", "tgt")),
            P(("src", "tgt")),
            P(),
            P(),
            P(None, None, ("src", "tgt"), None),
            P(),
            P(None, ("src", "tgt"), None),
            P(("src", "tgt"), None),
            P(),
            P(("src", "tgt")),
        ),
        out_specs=P(None, None, ("src", "tgt")),
        check_vma=False,
    )
```

time: 22 us -> 20.6 us (0.936)
  Pallas kernels: 20.1 us -> 18.7 us
    pallas_call x1, Pallas kernels: 20.1 us -> 18.7 us  [shards(): pl.pallas_call(functools.partial(kernel, S, T, N, src_bits, tgt_bits), ou...]
where the time goes in v2:
time: 20.6 us; the launch traced here: 20.4 us
  Pallas kernels  18.7 us (91%)
  local copies, waits for them, and re-layouts  1.67 us (8%)
    pallas_call x1, Pallas kernels, shards(): pl.pallas_call(functools.partial(kernel, S, T, N, src_bits, tgt_bits), ou...  18.7 us
    unnamed x1, local copies, waits for them, and re-layouts  1.67 us

profile of v2, /device:TPU:0, one launch (start us, length us, event | category | flops | bytes accessed | tf_op | source)
XLA Modules:
  0.0 20.4 jit_solution(5762111002783871036)
XLA Ops:
  0.0 18.7 %shard_map.100 = f32[2,16,2048]{2,1,0:T(8,128)} custom-call(f32[16,2048]{1,0:T(8,128)} %values_h.1, f32[16,128]{1,0:T(8,128)} %bitcast.2, bf16[64,64]{1,0:T(8,128)(2,1)} %leaf_h.1, bf16[11,2,64,64]{3,2,1,0:T(8,128)(2,1)} %lint_h.1, f32[11,3,32,64]{3,2,1,0:T(8,128)} %lphase_h.1, bf16[64,64]{1,0:T(8,128)(2,1)} %mint_h.1, f32[2,32,64]{2,1,0:T(8,128)} %mphase_h.1, ...), custom_call_target="tpu_custom_call" | custom-call | tf_op jit(solution)/shard_map/pallas_call | solution.py:387
  18.8 1.7 %copy.12 = f32[2,16,2048]{2,1,0:T(8,128)} copy(f32[2,16,2048]{2,1,0:T(8,128)} %shard_map.100) | data formatting | bytes 524288
